TPU v7x, 256 devices: a whole 4x4x8 slice. The times are simulated.
256 devices in a mesh: period: 128 (over z, x, y), half: 2 (over core).
Axes of the slice: x: 4, y: 4, z: 8, core: 2. Of those that a mesh axis runs over, the one named last changes fastest.
Arguments:
- probes: float32 [1024, 4, 512], P('period', None, 'half'), may hold values from -6 to 6
- footprints: bfloat16 [1024, 512, 512], P('period', None, 'half'), may hold values from -0.25 to 0.25
- lag_weights: float32 [1024, 4], P('period'), may hold values from 0.2 to 2
- owners: int32 [1024, 4], P('period'), may hold values from 0 to 127, all different within a row; in each aligned block of 8 rows (0 to 7, 8 to 15, ...) at most 2 rows name the same one
- window_tiles: int32 [1024, 2], P('period', 'half'), may hold values from 0 to 10
- coords: int32 [2, 3072], replicated, may hold values from 0 to 63
- temporal: float32 [128, 128], replicated, as said below
Outputs:
- coefficients: float32 [4, 4], replicated
- residual: float32 [1024, 4, 512], P('period', None, 'half')
Inputs may be any that keep to these rules, and one draw needn't show every extreme that they name: `owners`: each row names 4 different periods. Among the 8 rows of one index of period, no period is named more than 2 times, and one is named exactly 2 times. `temporal`: symmetric.
All inputs are finite; a program needn't handle non-finite values.
Results may differ from a plain program's by a relative error of at most 0.025.
Values may be sent and summed in bfloat16 or wider, within the bound.
No kernel may reach another device: no remote copies, remote signals or barrier semaphores. Data moves between devices by JAX's collectives and lax.ppermute only.
A program may use at most 64 MiB of HBM per device.

v0:
```python
import jax
import jax.numpy as jnp
from jax import lax
from jax.sharding import PartitionSpec as P

epsilon = 1e-06
kernel_scale = 0.05
kernel_length = 6.0
highest = lax.Precision.HIGHEST


def from_partner(block, axis, bit):
    count = lax.axis_size(axis)
    route = []
    for low in range(count):
        high = low | 1 << bit
        if high != low and high < count:
            route += [(low, high), (high, low)]
    return lax.ppermute(block, axis, route)


def body(probes, footprints, lag_weights, owners, window_tiles, coords, temporal):
    periods = lax.axis_size("period")
    half_index = lax.axis_index("half")
    block_count, top_count = owners.shape
    probe_count = probes.shape[1]
    sound_count = footprints.shape[1]
    window = footprints.shape[2]
    win_tiles = window // 128
    cell_count = coords.shape[1]
    half_cells = cell_count // 2
    tile_count = half_cells // 128
    group_cells = half_cells // periods
    total_rows = float(block_count * periods * sound_count)
    tiles = window_tiles[:, 0]
    tile_hot = (
        tiles[:, None, None] + jnp.arange(win_tiles, dtype=jnp.int32)[None, :, None]
        == jnp.arange(tile_count, dtype=jnp.int32)[None, None, :]
    ).astype(jnp.float32)
    own_coords = lax.dynamic_slice_in_dim(coords, half_index * half_cells, half_cells, 1)
    delta_x = own_coords[0][:, None] - coords[0][None, :]
    delta_y = own_coords[1][:, None] - coords[1][None, :]
    squared = (delta_x * delta_x + delta_y * delta_y).astype(jnp.float32)
    kernel_rows = (kernel_scale * jnp.exp(-jnp.sqrt(squared) / kernel_length)).reshape(
        periods, group_cells, cell_count
    )
    owner_hot = (owners[:, :, None] == jnp.arange(periods, dtype=jnp.int32)[None, None, :]).astype(
        jnp.float32
    )

    def add_half(piece_rows):
        return jnp.einsum(
            "bps,bsw->bpw", piece_rows, footprints, preferred_element_type=jnp.float32
        )

    def mix_periods(grouped_part):
        mixed_part = jnp.einsum("ts,sik->tik", temporal, grouped_part, precision=highest)
        return lax.all_to_all(mixed_part, "period", split_axis=0, concat_axis=0, tiled=True)

    def apply_operator(vector):
        vector_low = vector.astype(jnp.bfloat16)
        partial_value = add_half(lax.all_gather(vector_low, "half", axis=2, tiled=True))
        terms = lag_weights[:, :, None, None] * partial_value[:, None, :, :]
        term_tiles = terms.reshape(block_count, top_count, probe_count, win_tiles, 128)
        placed = jnp.einsum("bjt,bkpjl->bkptl", tile_hot, term_tiles, precision=highest)
        dense_terms = jnp.einsum("bkn,bkptl->nptl", owner_hot, placed, precision=highest)
        summed = lax.psum_scatter(
            dense_terms.reshape(periods, probe_count, half_cells),
            "period",
            scatter_dimension=0,
            tiled=True,
        )
        flux_half = summed[0]
        other_half = from_partner(flux_half, "half", 0)
        whole_flux = jnp.where(
            half_index == 0,
            jnp.concatenate([flux_half, other_half], axis=1),
            jnp.concatenate([other_half, flux_half], axis=1),
        )
        grouped = jnp.einsum("pc,gkc->gpk", whole_flux, kernel_rows, precision=highest)
        mixed_flux = mix_periods(
            lax.all_to_all(grouped, "period", split_axis=0, concat_axis=0, tiled=True)
        )
        field_low = (
            jnp.transpose(mixed_flux, (1, 0, 2))
            .reshape(probe_count, half_cells)
            .astype(jnp.bfloat16)
        )
        field_all = lax.all_gather(field_low[None], "period", axis=0, tiled=True)
        selected = jnp.einsum(
            "bkn,npc->bkpc",
            owner_hot.astype(jnp.bfloat16),
            field_all,
            preferred_element_type=jnp.float32,
        )
        selected = selected.reshape(block_count, top_count, probe_count, tile_count, 128)
        windows = jnp.einsum("bkptl,bjt->bkpjl", selected, tile_hot, precision=highest)
        windows = windows.astype(jnp.bfloat16).reshape(block_count, top_count, probe_count, window)
        products = jnp.einsum(
            "bkpw,bsw->bkps", windows, footprints, preferred_element_type=jnp.float32
        )
        sounded = jnp.einsum("bk,bkps->bps", lag_weights, products, precision=highest)
        return lax.psum_scatter(
            sounded.astype(jnp.bfloat16), "half", scatter_dimension=2, tiled=True
        ).astype(jnp.float32)

    def local_mean(values):
        return jnp.sum(values, axis=(0, 2))

    def lanczos_step(current, image):
        inner_sum = lax.psum(local_mean(current * image), ("period", "half"))
        alpha = inner_sum / total_rows
        remainder = image - alpha[None, :, None] * current
        square_sum = lax.psum(local_mean(remainder * remainder), ("period", "half"))
        beta = jnp.sqrt(square_sum / total_rows + epsilon)
        return (alpha, remainder, beta)

    start_sum = lax.psum(local_mean(probes * probes), ("period", "half"))
    first_q = probes / jnp.sqrt(start_sum / total_rows + epsilon)[None, :, None]
    image_one = apply_operator(first_q)
    alpha_one, rest_one, beta_one = lanczos_step(first_q, image_one)
    second_q = rest_one / beta_one[None, :, None]
    image_two = apply_operator(second_q) - beta_one[None, :, None] * first_q
    alpha_two, residual, beta_two = lanczos_step(second_q, image_two)
    coefficients = jnp.stack([alpha_one, beta_one, alpha_two, beta_two], axis=0)
    return (coefficients, residual)


def solution(mesh):
    in_specs = (
        P("period", None, "half"),
        P("period", None, "half"),
        P("period", None),
        P("period", None),
        P("period", "half"),
        P(),
        P(),
    )
    out_specs = (P(), P("period", None, "half"))
    return jax.shard_map(body, mesh=mesh, in_specs=in_specs, out_specs=out_specs, check_vma=False)
```

profile of v0, /device:TPU:1, one launch (start us, length us, event | category | flops | bytes accessed | tf_op | source)
XLA Modules:
  0.0 1305.8 jit_solution(13119377155676004425)
XLA Ops:
  7.2 1.0 multiply_reduce_fusion.3
  8.3 81.4 %psum.35 = f32[4]{0:T(128)S(1)} all-reduce(f32[4]{0:T(128)S(1)} %multiply_reduce_fusion.3), channel_id=1, replica_groups=mesh['period'=128,'half'=2] {'period','half'}, use_global_device_ids=true, to_apply=%region_1.0 | all-reduce | flops 4 | bytes 32 | tf_op jit(solution)/shard_map/psum | solution.py:118
  89.7 0.7 iota_add_fusion
  90.4 0.8 copy.24
  91.2 0.8 fusion.101
  92.0 2.5 all_gather.12
  94.9 0.8 convolution_bitcast_fusion.1
  95.7 4.4 fusion.38
  100.1 5.1 copy.26
  106.4 221.5 %all-reduce.5.cloned.1.call-done = f32[128,4,1536]{2,1,0:T(4,128)} async-done(((f32[128,4,1536]{2,1,0:T(4,128)}), f32[128,4,1536]{2,1,0:T(4,128)}) %all-reduce.5.cloned.1.call-update) | async-done | bytes 3145744
  328.0 1.4 dynamic-slice_bitcast_fusion.1
  329.4 4.9 collective-permute-start
  335.2 46.6 %fusion.32 = f32[128,4,12]{0,1,2:T(4,128)S(1)} fusion(s32[3072]{0:T(1024)S(1)} %bitcast.132, s32[128,12]{0,1:T(8,128)S(1)} %copy.23, s32[3072]{0:T(1024)S(1)} %bitcast.130, s32[128,12]{0,1:T(8,128)S(1)} %copy.22, f32[4,1536]{1,0:T(4,128)S(1)} %collective-permute-done, f32[4,1536]{1,0:T(4,128)S(1)} %dynamic-slice_bitcast_fusion.1, pred[]{:T(512)S(6)} %eq.36), kind=kOutput, calls=%fused_computation.35 | convolution fusion | flops 268996608 | bytes 110593 | tf_op jit(solution)/shard_map/pc,gkc->gpk/dot_general | solution.py:80
  382.0 23.7 %all_to_all.20 = f32[128,4,12]{2,1,0:T(4,128)S(1)} all-to-all(f32[128,4,12]{2,1,0:T(4,128)S(1)} %copy.27), channel_id=1, replica_groups=mesh['period'=128,'half'=2] {'period'}, dimensions={0} | all-to-all | bytes 49152 | tf_op jit(solution)/shard_map/all_to_all | solution.py:82
  406.4 17.2 %all_to_all.21 = bf16[128,4,12]{2,1,0:T(4,128)(2,1)S(1)} all-to-all(bf16[128,4,12]{2,1,0:T(4,128)(2,1)S(1)} %copy.29), channel_id=1, replica_groups=mesh['period'=128,'half'=2] {'period'}, dimensions={0} | all-to-all | bytes 24576 | tf_op jit(solution)/shard_map/all_to_all | solution.py:58
  423.7 0.8 convert_element_type.80
  424.8 94.2 %all-gather.3.cloned.1.call-done = bf16[128,4,1536]{2,1,0:T(4,128)(2,1)} async-done(((bf16[1,4,1536]{2,1,0:T(4,128)(2,1)}), bf16[128,4,1536]{2,1,0:T(4,128)(2,1)}) %all-gather.3.cloned.1.call-update) | async-done | bytes 1572880 | tf_op jit(solution)/shard_map/all_gather | solution.py:89
  519.0 2.0 fusion.24
  521.7 0.6 fusion.16
  522.3 0.6 fusion.42
  523.0 0.7 copy.52
  523.7 1.3 reshape.130
  525.1 16.9 %reduce-scatter.7.cloned.1.call-done = bf16[256,32]{1,0:T(8,128)(2,1)} async-done(((bf16[512,32]{1,0:T(8,128)(2,1)}), bf16[256,32]{1,0:T(8,128)(2,1)}) %reduce-scatter.7.cloned.1.call-update) | async-done | bytes 16400
  542.0 1.2 reshape.131
  543.7 77.4 %psum.36 = f32[4]{0:T(128)S(1)} all-reduce(f32[4]{0:T(128)S(1)} %fusion.68), channel_id=1, replica_groups=mesh['period'=128,'half'=2] {'period','half'}, use_global_device_ids=true, to_apply=%region_5.6 | all-reduce | flops 4 | bytes 32 | tf_op jit(solution)/shard_map/psum | solution.py:111
  621.3 73.1 %psum.37 = f32[4]{0:T(128)S(1)} all-reduce(f32[4]{0:T(128)S(1)} %multiply_reduce_fusion.2), channel_id=1, replica_groups=mesh['period'=128,'half'=2] {'period','half'}, use_global_device_ids=true, to_apply=%region_7.8 | all-reduce | flops 4 | bytes 32 | tf_op jit(solution)/shard_map/psum | solution.py:114
  694.5 2.2 all_gather.14
  697.1 0.8 convolution_bitcast_fusion
  697.9 4.4 fusion.36
  702.3 5.1 copy.34
  707.5 223.8 %all-reduce.7.cloned.1.call-done = f32[128,4,1536]{2,1,0:T(4,128)} async-done(((f32[128,4,1536]{2,1,0:T(4,128)}), f32[128,4,1536]{2,1,0:T(4,128)}) %all-reduce.7.cloned.1.call-update) | async-done | bytes 3145744
  931.3 1.4 dynamic-slice_bitcast_fusion
  932.7 4.9 collective-permute-start.1
  937.6 0.8 collective-permute-done.1
  938.5 46.6 %fusion.33 = f32[128,4,12]{0,1,2:T(4,128)S(1)} fusion(s32[3072]{0:T(1024)S(1)} %bitcast.133, s32[128,12]{0,1:T(8,128)S(1)} %copy.23, s32[3072]{0:T(1024)S(1)} %bitcast.131, s32[128,12]{0,1:T(8,128)S(1)} %copy.22, f32[4,1536]{1,0:T(4,128)S(1)} %collective-permute-done.1, f32[4,1536]{1,0:T(4,128)S(1)} %dynamic-slice_bitcast_fusion, pred[]{:T(512)S(6)} %eq.36), kind=kOutput, calls=%fused_computation.36 | convolution fusion | flops 268996608 | bytes 110593 | tf_op jit(solution)/shard_map/pc,gkc->gpk/dot_general | solution.py:80
  985.3 23.7 %all_to_all.22 = f32[128,4,12]{2,1,0:T(4,128)S(1)} all-to-all(f32[128,4,12]{2,1,0:T(4,128)S(1)} %copy.35), channel_id=1, replica_groups=mesh['period'=128,'half'=2] {'period'}, dimensions={0} | all-to-all | bytes 49152 | tf_op jit(solution)/shard_map/all_to_all | solution.py:82
  1009.7 17.2 %all_to_all.23 = bf16[128,4,12]{2,1,0:T(4,128)(2,1)S(1)} all-to-all(bf16[128,4,12]{2,1,0:T(4,128)(2,1)S(1)} %copy.37), channel_id=1, replica_groups=mesh['period'=128,'half'=2] {'period'}, dimensions={0} | all-to-all | bytes 24576 | tf_op jit(solution)/shard_map/all_to_all | solution.py:58
  1027.0 0.8 convert_element_type.88
  1027.9 94.5 %all-gather.5.cloned.1.call-done = bf16[128,4,1536]{2,1,0:T(4,128)(2,1)} async-done(((bf16[1,4,1536]{2,1,0:T(4,128)(2,1)}), bf16[128,4,1536]{2,1,0:T(4,128)(2,1)}) %all-gather.5.cloned.1.call-update) | async-done | bytes 1572880 | tf_op jit(solution)/shard_map/all_gather | solution.py:89
  1122.3 2.0 fusion.27
  1125.0 0.6 fusion.14
  1126.3 0.7 copy.54
  1127.0 1.3 reshape.132
  1128.4 16.9 %reduce-scatter.9.cloned.1.call-done = bf16[256,32]{1,0:T(8,128)(2,1)} async-done(((bf16[512,32]{1,0:T(8,128)(2,1)}), bf16[256,32]{1,0:T(8,128)(2,1)}) %reduce-scatter.9.cloned.1.call-update) | async-done | bytes 16400
  1145.3 1.2 reshape.133
  1147.0 77.4 %psum.38 = f32[4]{0:T(128)S(1)} all-reduce(f32[4]{0:T(128)S(1)} %multiply_reduce_fusion.1), channel_id=1, replica_groups=mesh['period'=128,'half'=2] {'period','half'}, use_global_device_ids=true, to_apply=%region_11.12 | all-reduce | flops 4 | bytes 32 | tf_op jit(solution)/shard_map/psum | solution.py:111
  1224.5 0.8 multiply_reduce_fusion
  1225.3 73.1 %psum.39 = f32[4]{0:T(128)S(1)} all-reduce(f32[4]{0:T(128)S(1)} %get-tuple-element.4), channel_id=1, replica_groups=mesh['period'=128,'half'=2] {'period','half'}, use_global_device_ids=true, to_apply=%region_13.14 | all-reduce | flops 4 | bytes 32 | tf_op jit(solution)/shard_map/psum | solution.py:114
  (64 shorter events, 9.1 us)
Async XLA Ops:
  7.2 87.3 %copy-start = (bf16[8,512,256]{2,1,0:T(8,128)(2,1)S(1)}, bf16[8,512,256]{2,1,0:T(8,128)(2,1)}, u32[]{:S(2)}) copy-start(bf16[8,512,256]{2,1,0:T(8,128)(2,1)} %param.8) | copy-start | bytes 6291460
  7.2 88.5 %copy-start.3 = (s32[8,4]{0,1:T(4,128)S(1)}, s32[8,4]{0,1:T(4,128)}, u32[]{:S(2)}) copy-start(s32[8,4]{0,1:T(4,128)} %param.10) | copy-start | bytes 388
  7.2 320.8 %all-reduce.5.cloned.1.call-start = ((), (), s32[]{:S(2)}) async-start(), calls=%async_computation.10 | async-start | bytes 6291456
  105.2 0.7 copy-start.5
  105.2 229.1 %copy-start.2 = (s32[2,3072]{1,0:T(2,128)S(1)}, s32[2,3072]{1,0:T(2,128)}, u32[]{:S(2)}) copy-start(s32[2,3072]{1,0:T(2,128)} %param.12) | copy-start | bytes 73732
  105.2 413.8 %all-gather.3.cloned.1.call-start = ((), (), s32[]{:S(2)}) async-start(), calls=%async_computation.6 | async-start | bytes 1585152 | tf_op jit(solution)/shard_map/all_gather | solution.py:89
  329.4 5.8 collective-permute-start
  335.2 70.5 %copy-start.1 = (f32[128,128]{1,0:T(8,128)S(1)}, f32[128,128]{1,0:T(8,128)}, u32[]{:S(2)}) copy-start(f32[128,128]{1,0:T(8,128)} %param.13) | copy-start | bytes 196612
  335.2 89.6 %copy-start.4 = (f32[8,4]{0,1:T(4,128)S(1)}, f32[8,4]{0,1:T(4,128)}, u32[]{:S(2)}) copy-start(f32[8,4]{0,1:T(4,128)} %param.9) | copy-start | bytes 388
  424.5 117.5 %reduce-scatter.7.cloned.1.call-start = ((), (), s32[]{:S(2)}) async-start(), calls=%async_computation.8 | async-start | bytes 196608
  525.0 406.2 %all-reduce.7.cloned.1.call-start = ((), (), s32[]{:S(2)}) async-start(), calls=%async_computation.11 | async-start | bytes 6291456
  707.4 414.9 %all-gather.5.cloned.1.call-start = ((), (), s32[]{:S(2)}) async-start(), calls=%async_computation.7 | async-start | bytes 1585152 | tf_op jit(solution)/shard_map/all_gather | solution.py:89
  932.7 5.8 collective-permute-start.1
  1027.8 117.5 %reduce-scatter.9.cloned.1.call-start = ((), (), s32[]{:S(2)}) async-start(), calls=%async_computation.9 | async-start | bytes 196608
Sparse Core Ops, SparseCore 0:
  105.3 222.5 all-reduce.4
  424.6 94.3 all-gather.2
  525.2 16.7 reduce-scatter.6
  707.5 223.6 all-reduce.6
  1027.9 94.3 all-gather.4
  1128.5 16.7 reduce-scatter.8
where the time goes:
time: 1310 us
  waiting for transfers between devices  669 us (51%)
  blocking collectives  469 us (36%)
  matrix products  113 us (9%)
  local copies, waits for them, and re-layouts  25.2 us (2%)
  between operations  14.4 us (1%)
    unnamed x10, waiting for transfers between devices  479 us
    all_gather x2, waiting for transfers between devices, apply_operator(): field_all = lax.all_gather(field_low[None], 'period', axis=0, tiled=True)  189 us
    psum x2, blocking collectives, lanczos_step(): inner_sum = lax.psum(local_mean(current * image), ('period', 'half'))  155 us
    psum x2, blocking collectives, lanczos_step(): square_sum = lax.psum(local_mean(remainder * remainder), ('period', 'half'))  146 us
    dot_general x2, matrix products, apply_operator(): jnp.einsum('pc,gkc->gpk', whole_flux, kernel_rows, precision=highest)  93.3 us
    psum x1, blocking collectives, body(): start_sum = lax.psum(local_mean(probes * probes), ('period', 'half'))  81.4 us
    all_to_all x2, blocking collectives, apply_operator(): lax.all_to_all(grouped, 'period', split_axis=0, concat_axis=0, tiled=True)  47.4 us
    all_to_all x2, blocking collectives, mix_periods(): lax.all_to_all(mixed_part, 'period', split_axis=0, concat_axis=0, tiled=T...  34.5 us
  transfers between devices with their start and end apart: 8, of which 8 were waited for; matrix products, arithmetic and copies ran while one was open for 0% of the time, Pallas kernels for 0%

commit v1 on v0

--- a/solution.py
+++ b/solution.py
@@ -115,7 +115,9 @@
         beta = jnp.sqrt(square_sum / total_rows + epsilon)
         return (alpha, remainder, beta)
 
-    start_sum = lax.psum(local_mean(probes * probes), ("period", "half"))
+    start_sum = local_mean(probes * probes)
+    for d in ("half", "period"):
+        start_sum = lax.psum(start_sum, d)
     first_q = probes / jnp.sqrt(start_sum / total_rows + epsilon)[None, :, None]
     image_one = apply_operator(first_q)
     alpha_one, rest_one, beta_one = lanczos_step(first_q, image_one)

time: 1310 us -> 1580 us (1.21)
  blocking collectives: 469 us -> 743 us
    psum x1 -> x2, blocking collectives: 81.4 us -> 301 us  [body(): start_sum = lax.psum(start_sum, d)]
    all_gather x2, blocking collectives: 4.65 us -> 59.3 us  [apply_operator(): lax.all_gather(vector_low, 'half', axis=2, tiled=True)]
where the time goes in v1:
time: 1580 us
  blocking collectives  743 us (47%)
  waiting for transfers between devices  666 us (42%)
  matrix products  113 us (7%)
  local copies, waits for them, and re-layouts  25.2 us (2%)
    unnamed x10, waiting for transfers between devices  476 us
    psum x2, blocking collectives, body(): start_sum = lax.psum(start_sum, d)  301 us
    all_gather x2, waiting for transfers between devices, apply_operator(): field_all = lax.all_gather(field_low[None], 'period', axis=0, tiled=True)  189 us
    psum x2, blocking collectives, lanczos_step(): inner_sum = lax.psum(local_mean(current * image), ('period', 'half'))  155 us
    psum x2, blocking collectives, lanczos_step(): square_sum = lax.psum(local_mean(remainder * remainder), ('period', 'half'))  146 us
    dot_general x2, matrix products, apply_operator(): jnp.einsum('pc,gkc->gpk', whole_flux, kernel_rows, precision=highest)  93.3 us
    all_gather x2, blocking collectives, apply_operator(): lax.all_gather(vector_low, 'half', axis=2, tiled=True)  59.3 us
    all_to_all x2, blocking collectives, apply_operator(): lax.all_to_all(grouped, 'period', split_axis=0, concat_axis=0, tiled=True)  47.4 us
  transfers between devices with their start and end apart: 8, of which 8 were waited for; matrix products, arithmetic and copies ran while one was open for 0% of the time, Pallas kernels for 0%

profile of v1, /device:TPU:1, one launch (start us, length us, event | category | flops | bytes accessed | tf_op | source)
XLA Modules:
  0.0 1577.1 jit_solution(17781988904346557545)
XLA Ops:
  7.2 1.0 multiply_reduce_fusion.3
  8.3 5.3 psum.42
  13.6 295.7 %psum.43 = f32[4]{0:T(128)S(1)} all-reduce(f32[4]{0:T(128)S(1)} %psum.42), channel_id=1, replica_groups=mesh['period'=128,'half'=2] {'period'}, use_global_device_ids=true, to_apply=%region_2.0 | all-reduce | flops 4 | bytes 32 | tf_op jit(solution)/shard_map/psum | solution.py:120
  309.3 0.7 iota_add_fusion
  310.1 0.8 copy.24
  310.8 0.8 fusion.101
  311.7 57.1 %all_gather.12 = bf16[8,4,512]{2,1,0:T(4,128)(2,1)S(1)} all-gather(bf16[8,4,256]{2,1,0:T(4,128)(2,1)S(1)} %get-tuple-element.8), channel_id=1, replica_groups=mesh['period'=128,'half'=2] {'half'}, dimensions={2}, use_global_device_ids=true | all-gather | bytes 49152 | tf_op jit(solution)/shard_map/all_gather | solution.py:62
  369.2 0.8 convolution_bitcast_fusion.1
  370.0 4.4 fusion.38
  374.3 5.1 copy.26
  380.7 218.5 %all-reduce.5.cloned.1.call-done = f32[128,4,1536]{2,1,0:T(4,128)} async-done(((f32[128,4,1536]{2,1,0:T(4,128)}), f32[128,4,1536]{2,1,0:T(4,128)}) %all-reduce.5.cloned.1.call-update) | async-done | bytes 3145744
  599.3 1.4 dynamic-slice_bitcast_fusion.1
  600.6 4.9 collective-permute-start
  606.4 46.6 %fusion.32 = f32[128,4,12]{0,1,2:T(4,128)S(1)} fusion(s32[3072]{0:T(1024)S(1)} %bitcast.132, s32[128,12]{0,1:T(8,128)S(1)} %copy.23, s32[3072]{0:T(1024)S(1)} %bitcast.130, s32[128,12]{0,1:T(8,128)S(1)} %copy.22, f32[4,1536]{1,0:T(4,128)S(1)} %collective-permute-done, f32[4,1536]{1,0:T(4,128)S(1)} %dynamic-slice_bitcast_fusion.1, pred[]{:T(512)S(6)} %eq.36), kind=kOutput, calls=%fused_computation.35 | convolution fusion | flops 268996608 | bytes 110593 | tf_op jit(solution)/shard_map/pc,gkc->gpk/dot_general | solution.py:80
  653.3 23.7 %all_to_all.20 = f32[128,4,12]{2,1,0:T(4,128)S(1)} all-to-all(f32[128,4,12]{2,1,0:T(4,128)S(1)} %copy.27), channel_id=1, replica_groups=mesh['period'=128,'half'=2] {'period'}, dimensions={0} | all-to-all | bytes 49152 | tf_op jit(solution)/shard_map/all_to_all | solution.py:82
  677.7 17.2 %all_to_all.21 = bf16[128,4,12]{2,1,0:T(4,128)(2,1)S(1)} all-to-all(bf16[128,4,12]{2,1,0:T(4,128)(2,1)S(1)} %copy.29), channel_id=1, replica_groups=mesh['period'=128,'half'=2] {'period'}, dimensions={0} | all-to-all | bytes 24576 | tf_op jit(solution)/shard_map/all_to_all | solution.py:58
  695.0 0.8 convert_element_type.80
  696.1 94.2 %all-gather.3.cloned.1.call-done = bf16[128,4,1536]{2,1,0:T(4,128)(2,1)} async-done(((bf16[1,4,1536]{2,1,0:T(4,128)(2,1)}), bf16[128,4,1536]{2,1,0:T(4,128)(2,1)}) %all-gather.3.cloned.1.call-update) | async-done | bytes 1572880 | tf_op jit(solution)/shard_map/all_gather | solution.py:89
  790.3 2.0 fusion.24
  793.0 0.6 fusion.16
  794.3 0.7 copy.52
  795.0 1.3 reshape.130
  796.4 16.9 %reduce-scatter.7.cloned.1.call-done = bf16[256,32]{1,0:T(8,128)(2,1)} async-done(((bf16[512,32]{1,0:T(8,128)(2,1)}), bf16[256,32]{1,0:T(8,128)(2,1)}) %reduce-scatter.7.cloned.1.call-update) | async-done | bytes 16400
  813.3 1.2 reshape.131
  815.0 77.4 %psum.44 = f32[4]{0:T(128)S(1)} all-reduce(f32[4]{0:T(128)S(1)} %fusion.68), channel_id=1, replica_groups=mesh['period'=128,'half'=2] {'period','half'}, use_global_device_ids=true, to_apply=%region_6.7 | all-reduce | flops 4 | bytes 32 | tf_op jit(solution)/shard_map/psum | solution.py:111
  892.6 73.1 %psum.45 = f32[4]{0:T(128)S(1)} all-reduce(f32[4]{0:T(128)S(1)} %multiply_reduce_fusion.2), channel_id=1, replica_groups=mesh['period'=128,'half'=2] {'period','half'}, use_global_device_ids=true, to_apply=%region_8.9 | all-reduce | flops 4 | bytes 32 | tf_op jit(solution)/shard_map/psum | solution.py:114
  965.8 2.2 all_gather.14
  968.4 0.8 convolution_bitcast_fusion
  969.2 4.4 fusion.36
  973.6 5.1 copy.34
  978.8 223.8 %all-reduce.7.cloned.1.call-done = f32[128,4,1536]{2,1,0:T(4,128)} async-done(((f32[128,4,1536]{2,1,0:T(4,128)}), f32[128,4,1536]{2,1,0:T(4,128)}) %all-reduce.7.cloned.1.call-update) | async-done | bytes 3145744
  1202.6 1.4 dynamic-slice_bitcast_fusion
  1204.0 4.9 collective-permute-start.1
  1208.9 0.8 collective-permute-done.1
  1209.8 46.6 %fusion.33 = f32[128,4,12]{0,1,2:T(4,128)S(1)} fusion(s32[3072]{0:T(1024)S(1)} %bitcast.133, s32[128,12]{0,1:T(8,128)S(1)} %copy.23, s32[3072]{0:T(1024)S(1)} %bitcast.131, s32[128,12]{0,1:T(8,128)S(1)} %copy.22, f32[4,1536]{1,0:T(4,128)S(1)} %collective-permute-done.1, f32[4,1536]{1,0:T(4,128)S(1)} %dynamic-slice_bitcast_fusion, pred[]{:T(512)S(6)} %eq.36), kind=kOutput, calls=%fused_computation.36 | convolution fusion | flops 268996608 | bytes 110593 | tf_op jit(solution)/shard_map/pc,gkc->gpk/dot_general | solution.py:80
  1256.6 23.7 %all_to_all.22 = f32[128,4,12]{2,1,0:T(4,128)S(1)} all-to-all(f32[128,4,12]{2,1,0:T(4,128)S(1)} %copy.35), channel_id=1, replica_groups=mesh['period'=128,'half'=2] {'period'}, dimensions={0} | all-to-all | bytes 49152 | tf_op jit(solution)/shard_map/all_to_all | solution.py:82
  1281.0 17.2 %all_to_all.23 = bf16[128,4,12]{2,1,0:T(4,128)(2,1)S(1)} all-to-all(bf16[128,4,12]{2,1,0:T(4,128)(2,1)S(1)} %copy.37), channel_id=1, replica_groups=mesh['period'=128,'half'=2] {'period'}, dimensions={0} | all-to-all | bytes 24576 | tf_op jit(solution)/shard_map/all_to_all | solution.py:58
  1298.3 0.8 convert_element_type.88
  1299.2 94.5 %all-gather.5.cloned.1.call-done = bf16[128,4,1536]{2,1,0:T(4,128)(2,1)} async-done(((bf16[1,4,1536]{2,1,0:T(4,128)(2,1)}), bf16[128,4,1536]{2,1,0:T(4,128)(2,1)}) %all-gather.5.cloned.1.call-update) | async-done | bytes 1572880 | tf_op jit(solution)/shard_map/all_gather | solution.py:89
  1393.6 2.0 fusion.27
  1396.3 0.6 fusion.14
  1397.6 0.7 copy.54
  1398.3 1.3 reshape.132
  1399.7 16.9 %reduce-scatter.9.cloned.1.call-done = bf16[256,32]{1,0:T(8,128)(2,1)} async-done(((bf16[512,32]{1,0:T(8,128)(2,1)}), bf16[256,32]{1,0:T(8,128)(2,1)}) %reduce-scatter.9.cloned.1.call-update) | async-done | bytes 16400
  1416.6 1.2 reshape.133
  1418.4 77.4 %psum.46 = f32[4]{0:T(128)S(1)} all-reduce(f32[4]{0:T(128)S(1)} %multiply_reduce_fusion.1), channel_id=1, replica_groups=mesh['period'=128,'half'=2] {'period','half'}, use_global_device_ids=true, to_apply=%region_12.13 | all-reduce | flops 4 | bytes 32 | tf_op jit(solution)/shard_map/psum | solution.py:111
  1495.8 0.8 multiply_reduce_fusion
  1496.6 73.1 %psum.47 = f32[4]{0:T(128)S(1)} all-reduce(f32[4]{0:T(128)S(1)} %get-tuple-element.4), channel_id=1, replica_groups=mesh['period'=128,'half'=2] {'period','half'}, use_global_device_ids=true, to_apply=%region_14.15 | all-reduce | flops 4 | bytes 32 | tf_op jit(solution)/shard_map/psum | solution.py:114
  (65 shorter events, 9.7 us)
Async XLA Ops:
  7.2 361.6 %copy-start = (bf16[8,512,256]{2,1,0:T(8,128)(2,1)S(1)}, bf16[8,512,256]{2,1,0:T(8,128)(2,1)}, u32[]{:S(2)}) copy-start(bf16[8,512,256]{2,1,0:T(8,128)(2,1)} %param.8) | copy-start | bytes 6291460
  7.2 362.8 %copy-start.3 = (s32[8,4]{0,1:T(4,128)S(1)}, s32[8,4]{0,1:T(4,128)}, u32[]{:S(2)}) copy-start(s32[8,4]{0,1:T(4,128)} %param.10) | copy-start | bytes 388
  7.2 592.1 %all-reduce.5.cloned.1.call-start = ((), (), s32[]{:S(2)}) async-start(), calls=%async_computation.10 | async-start | bytes 6291456
  379.5 0.7 copy-start.5
  379.5 226.1 %copy-start.2 = (s32[2,3072]{1,0:T(2,128)S(1)}, s32[2,3072]{1,0:T(2,128)}, u32[]{:S(2)}) copy-start(s32[2,3072]{1,0:T(2,128)} %param.12) | copy-start | bytes 73732
  379.5 410.8 %all-gather.3.cloned.1.call-start = ((), (), s32[]{:S(2)}) async-start(), calls=%async_computation.6 | async-start | bytes 1585152 | tf_op jit(solution)/shard_map/all_gather | solution.py:89
  600.6 5.8 collective-permute-start
  606.4 70.5 %copy-start.1 = (f32[128,128]{1,0:T(8,128)S(1)}, f32[128,128]{1,0:T(8,128)}, u32[]{:S(2)}) copy-start(f32[128,128]{1,0:T(8,128)} %param.13) | copy-start | bytes 196612
  606.4 89.6 %copy-start.4 = (f32[8,4]{0,1:T(4,128)S(1)}, f32[8,4]{0,1:T(4,128)}, u32[]{:S(2)}) copy-start(f32[8,4]{0,1:T(4,128)} %param.9) | copy-start | bytes 388
  695.8 117.5 %reduce-scatter.7.cloned.1.call-start = ((), (), s32[]{:S(2)}) async-start(), calls=%async_computation.8 | async-start | bytes 196608
  796.3 406.3 %all-reduce.7.cloned.1.call-start = ((), (), s32[]{:S(2)}) async-start(), calls=%async_computation.11 | async-start | bytes 6291456
  978.7 414.9 %all-gather.5.cloned.1.call-start = ((), (), s32[]{:S(2)}) async-start(), calls=%async_computation.7 | async-start | bytes 1585152 | tf_op jit(solution)/shard_map/all_gather | solution.py:89
  1204.0 5.8 collective-permute-start.1
  1299.1 117.5 %reduce-scatter.9.cloned.1.call-start = ((), (), s32[]{:S(2)}) async-start(), calls=%async_computation.9 | async-start | bytes 196608
Sparse Core Ops, SparseCore 0:
  379.6 219.6 all-reduce.4
  695.9 94.3 all-gather.2
  796.5 16.7 reduce-scatter.6
  978.8 223.7 all-reduce.6
  1299.2 94.3 all-gather.4
  1399.8 16.7 reduce-scatter.8
